TPU v7x, 256 devices: a whole 4x4x8 slice. The times are simulated.
256 devices in a mesh: section: 16 (over x_hi, y, core), tm: 16 (over z, x_lo).
Axes of the slice: x: 4 (x_hi: 2, x_lo: 2; x = x_hi * 2 + x_lo), y: 4, z: 8, core: 2. Of those that a mesh axis runs over, the one named last changes fastest.
Arguments:
- fwd_input: bfloat16 [16, 2048, 1536], P('section', 'tm'), may hold values from -6 to 6
- saved_input: bfloat16 [16, 2048, 1536], P('section', 'tm'), may hold values from -6 to 6
- grad_in: bfloat16 [16, 2048, 1536], P('section', 'tm'), may hold values from -6 to 6
- gain: float32 [16, 1536], P('section'), may hold values from 0.25 to 1.75
- kernel: float32 [16, 31, 1536], P('section'), may hold values from -1 to 1
- w_out: bfloat16 [16, 1536, 1536], P('section', 'tm'), may hold values from -0.15625 to 0.15625
- lengths: int32 [32], replicated, may hold values from 1 to 2048, 49152 in all
- plan: int32 [16, 2], P('section'), may hold values from 0 to 31
Outputs:
- passed_activation: bfloat16 [16, 2048, 1536], P('section', 'tm')
- passed_gradient: bfloat16 [16, 2048, 1536], P('section', 'tm')
- weight_grad: float32 [16, 1536, 1536], P('section', 'tm')
- kernel_grad: float32 [16, 31, 1536], P('section')
- gain_grad: float32 [16, 1536], P('section')
Inputs may be any that keep to these rules, and one draw needn't show every extreme that they name: `lengths`: 32 valid counts summing to 49152, the largest exactly 2048. `plan`: indices into lengths.
All inputs are finite; a program needn't handle non-finite values.
Results may differ from a plain program's by a relative error of at most 0.017.
Values may be sent and summed in bfloat16 or wider, within the bound.
No kernel may reach another device: no remote copies, remote signals or barrier semaphores. Data moves between devices by JAX's collectives and lax.ppermute only.
A program may use at most 64 MiB of HBM per device.

v0:
```python
import jax
import jax.numpy as jnp
from jax import lax
from jax.sharding import PartitionSpec as P

KW = 31


def extended(array, sides, width):
    for axis, dim in sides:
        size, length = (lax.axis_size(axis), array.shape[dim])
        up = [(i, (i + 1) % size) for i in range(size - 1)]
        down = [(j, i) for i, j in up]
        last = lax.slice_in_dim(array, length - width, length, axis=dim)
        first = lax.slice_in_dim(array, 0, width, axis=dim)
        before = lax.ppermute(last, axis, up)
        after = lax.ppermute(first, axis, down)
        array = jnp.concatenate([before, array, after], axis=dim)
    return array


def from_behind(array, axis, by):
    length = lax.axis_size(axis)
    pairs = [(i, i + by) for i in range(length) if 0 <= i + by < length]
    return lax.ppermute(array, axis, pairs)


def normalize(values):
    center = values - jnp.mean(values, axis=-1, keepdims=True)
    inverse = lax.rsqrt(jnp.mean(center * center, axis=-1, keepdims=True) + 1e-05)
    return (center * inverse, inverse)


def swish_act(values):
    return values * jax.nn.sigmoid(values)


def conv_taps(padded, kernel_rows, frames):
    running = jnp.zeros(padded.shape[:-2] + (frames, padded.shape[-1]), jnp.float32)
    for tap_index in range(KW):
        running = running + kernel_rows[tap_index] * padded[..., tap_index : tap_index + frames, :]
    return running


def per_device(fwd_input, saved_input, grad_in, gain, kernel, w_out, lengths, plan):
    frames = fwd_input.shape[1]
    pieces = lax.axis_size("tm")
    margin = KW // 2
    factor = float(frames * pieces) ** (-0.5)
    position = lax.axis_index("tm") * frames + lax.iota(jnp.int32, frames)
    slot_ids = lax.iota(jnp.int32, lengths.shape[0])
    fwd_len = jnp.sum(jnp.where(slot_ids == plan[0, 0], lengths, 0))
    bwd_len = jnp.sum(jnp.where(slot_ids == plan[0, 1], lengths, 0))
    fwd_mask = (position < fwd_len).astype(jnp.float32)[:, None]
    bwd_mask = (position < bwd_len).astype(jnp.float32)[:, None]
    gain_row = gain[0]
    kernel_rows = kernel[0]
    w_rows = w_out[0]
    upstream = grad_in[0]
    fwd_float = fwd_input[0].astype(jnp.float32)
    fwd_hat, unused_inverse = normalize(fwd_float)
    saved_hat, inverse = normalize(saved_input[0].astype(jnp.float32))
    conv_fwd = (fwd_hat * gain_row * fwd_mask).astype(jnp.bfloat16)
    conv_saved = (saved_hat * gain_row * bwd_mask).astype(jnp.bfloat16)
    padded = extended(jnp.stack([conv_fwd, conv_saved]), (("tm", 1),), margin)
    padded_float = padded.astype(jnp.float32)
    mixed_all = conv_taps(padded_float, kernel_rows, frames)
    mixed_saved = mixed_all[1]
    hidden_fwd = swish_act(mixed_all[0]).astype(jnp.bfloat16)
    hidden_saved = swish_act(mixed_saved).astype(jnp.bfloat16)
    columns = hidden_fwd
    product = jnp.dot(
        columns,
        lax.all_gather(w_rows, "tm", axis=0, tiled=True),
        preferred_element_type=jnp.float32,
    )
    hidden_grad = lax.dot_general(
        upstream,
        lax.all_gather(w_rows, "tm", axis=0, tiled=True),
        (((1,), (1,)), ((), ())),
        preferred_element_type=jnp.float32,
    )
    output = (fwd_float + product).astype(jnp.bfloat16)
    passed_activation = from_behind(output[None], "section", 1)
    gate_sig = jax.nn.sigmoid(mixed_saved)
    conv_grad = (hidden_grad * (gate_sig + mixed_saved * gate_sig * (1.0 - gate_sig))).astype(
        jnp.bfloat16
    )
    pad_grad = extended(conv_grad, (("tm", 0),), margin).astype(jnp.float32)
    input_grad = jnp.zeros((frames, conv_grad.shape[1]), jnp.float32)
    for tap_index in range(KW):
        begin_at = 2 * margin - tap_index
        input_grad = input_grad + kernel_rows[tap_index] * pad_grad[begin_at : begin_at + frames]
    grad_float = conv_grad.astype(jnp.float32)
    pad_saved = padded_float[1]
    kernel_local = (
        jnp.stack(
            [
                jnp.sum(grad_float * pad_saved[tap_index : tap_index + frames], axis=0)
                for tap_index in range(KW)
            ]
        )
        * factor
    )
    norm_grad = input_grad * bwd_mask
    gain_local = jnp.sum(norm_grad * saved_hat, axis=0) * factor
    kernel_grad, gain_grad = (
        lax.psum(kernel_local.astype(jnp.bfloat16), "tm").astype(jnp.float32),
        lax.psum(gain_local.astype(jnp.bfloat16), "tm").astype(jnp.float32),
    )
    columns = hidden_saved
    partial_value = (
        lax.dot_general(
            columns, upstream, (((0,), (0,)), ((), ())), preferred_element_type=jnp.float32
        )
        * factor
    )
    weight_grad = lax.psum_scatter(
        lax.optimization_barrier(partial_value.astype(jnp.bfloat16))
        .astype(jnp.float32)
        .astype(jnp.bfloat16),
        "tm",
        scatter_dimension=0,
        tiled=True,
    ).astype(jnp.float32)
    hat_grad = norm_grad * gain_row
    input_back = upstream.astype(jnp.float32) + inverse * (
        hat_grad
        - jnp.mean(hat_grad, axis=-1, keepdims=True)
        - saved_hat * jnp.mean(hat_grad * saved_hat, axis=-1, keepdims=True)
    )
    passed_gradient = from_behind(input_back.astype(jnp.bfloat16)[None], "section", -1)
    return (
        passed_activation,
        passed_gradient,
        weight_grad[None],
        kernel_grad[None],
        gain_grad[None],
    )


def solution(mesh):
    placed = (
        P("section", "tm", None),
        P("section", "tm", None),
        P("section", "tm", None),
        P("section", None),
        P("section", None, None),
        P("section", "tm", None),
        P(),
        P("section", None),
    )
    return jax.shard_map(
        per_device,
        mesh=mesh,
        in_specs=placed,
        out_specs=(
            P("section", "tm", None),
            P("section", "tm", None),
            P("section", "tm", None),
            P("section", None, None),
            P("section", None),
        ),
        check_vma=False,
    )
```

profile of v0, /device:TPU:42, one launch (start us, length us, event | category | flops | bytes accessed | tf_op | source)
XLA Modules:
  0.0 398.9 jit_solution(7578486727265539355)
XLA Ops:
  7.2 0.0 copy-start.1
  7.2 0.0 copy-start
  7.2 0.0 all-gather.3.cloned.1.call-start
  7.2 0.7 all-gather.3.cloned.1.call-update
  7.9 0.0 all-reduce.2.cloned.1.call-start
  8.0 0.7 reduce.3
  8.7 1.3 fusion.152
  10.0 2.6 fusion.146
  12.6 1.3 compare_convert_fusion
  13.9 0.0 copy-start.69
  13.9 1.1 convert_reduce_fusion.1
  15.0 1.1 convert_reduce_fusion
  16.2 1.2 fusion.52
  17.5 0.3 fusion.73
  17.7 0.4 fusion.56
  18.2 3.8 collective-permute-start
  22.0 2.0 collective-permute-start.1
  24.1 0.3 slice_reduce_fusion.30
  24.6 0.2 slice_reduce_fusion.29
  24.9 0.0 copy-start.61
  24.9 0.0 copy-start.63
  24.9 0.6 collective-permute-done
  25.5 6.0 %collective-permute-done.1 = bf16[2,15,1536]{2,1,0:T(8,128)(2,1)S(1)} collective-permute-done((bf16[2,15,1536]{2,1,0:T(8,128)(2,1)S(1)}, bf16[2,15,1536]{2,1,0:T(8,128)(2,1)S(1)}, u32[]{:S(2)}, u32[]{:S(2)}) %collective-permute-start.1) | collective-permute-done | bytes 92192 | tf_op jit(solution)/shard_map/ppermute | solution.py:17
  31.5 0.3 maximum_convert_fusion
  32.1 0.0 copy-start.3
  32.1 6.8 %fusion.20 = f32[2,128,1536]{2,1,0:T(8,128)} fusion(f32[2,158,1536]{2,1,0:T(8,128)S(1)} %maximum_convert_fusion, f32[1536]{0:T(1024)S(1)} %get-tuple-element.68, f32[1536]{0:T(1024)S(1)} %get-tuple-element.69, f32[1536]{0:T(1024)S(1)} %get-tuple-element.40, f32[1536]{0:T(1024)S(1)} %get-tuple-element.41, f32[1536]{0:T(1024)S(1)} %get-tuple-element.42, ...), kind=kLoop, calls=%fused_computation.43 | loop fusion | flops 23986176 | bytes 50522112 | tf_op jit(solution)/shard_map/add | solution.py:41
  38.9 86.8 %all-gather.3.cloned.1.call-done = bf16[1,1536,1536]{2,1,0:T(8,128)(2,1)} async-done(((bf16[1,96,1536]{2,1,0:T(8,128)(2,1)}), bf16[1,1536,1536]{2,1,0:T(8,128)(2,1)}) %all-gather.3.cloned.1.call-update) | async-done | bytes 4718608 | tf_op jit(solution)/shard_map/all_gather | solution.py:74
  125.8 5.5 %fusion.103 = (f32[1536]{0:T(1024)S(1)}, f32[1536]{0:T(1024)S(1)}, f32[1536]{0:T(1024)S(1)}, f32[1536]{0:T(1024)S(1)}, f32[1536]{0:T(1024)S(1)}, /*index=5*/f32[...) fusion(f32[2,158,1536]{2,1,0:T(8,128)S(1)} %maximum_convert_fus, ...), kind=kOutput, calls=%fused_computation.163 | convolution fusion | flops 611037696 | bytes 16594944 | tf_op jit(solution)/shard_map/dot_general | solution.py:77
  131.2 2.0 fusion.104
  133.6 0.6 stack.113
  134.2 0.6 stack.114
  134.8 0.6 stack.115
  135.4 0.6 stack.116
  136.0 0.6 stack.117
  136.6 0.6 stack.118
  137.2 0.6 stack.119
  137.8 1.8 stack.133
  139.6 0.8 broadcast_in_dim.42
  140.3 0.0 all-reduce.2.cloned.1.call-update
  140.4 0.0 reduce-scatter.2.cloned.1.call-start
  140.4 3.6 fusion
  144.0 0.0 reduce-scatter.2.cloned.1.call-update
  144.1 2.4 collective-permute-start.3
  146.8 0.0 copy-start.62
  146.8 0.0 copy-start.64
  146.9 3.5 collective-permute-start.4
  150.4 3.9 fusion.17
  154.3 2.1 collective-permute-start.2
  156.4 0.0 collective-permute-done.3
  156.4 0.0 collective-permute-done.4
  156.4 0.1 maximum_convert_fusion.1
  156.9 5.1 %fusion.72 = (f32[1536]{0:T(1024)S(1)}, f32[128]{0:T(128)S(1)}, f32[128]{0:T(128)S(1)}, f32[128,1536]{1,0:T(8,128)S(1)}) fusion(bf16[1,128,1536]{2,1,0:T(8,128)(2,1)S(1)} %copy-done, f32[128]{0:T(128)S(1)} %copy-done.68, f32[128]{0:T(128)S(1)} %copy-done.66, f32[1536]{0:T(1024)S(1)} %reduce.3, f32[128]{0:T(128)S(1)} %copy-done.70, ...), kind=kLoop, calls=%fused_computation.132 | loop fusion | flops 13957376 | bytes 25764352 | tf_op jit(solution)/shard_map/reduce_sum | solution.py:106
  162.0 0.4 fusion.141
  162.4 3.6 collective-permute-start.5
  166.1 31.3 %psum.15 = bf16[1,1536]{1,0:T(2,128)(2,1)S(1)} all-reduce(bf16[1,1536]{1,0:T(2,128)(2,1)S(1)} %broadcast_in_dim.44), channel_id=1, replica_groups=mesh['section'=16,'tm'=16] {'tm'}, use_global_device_ids=true, to_apply=%region_42.43 | all-reduce | flops 1536 | bytes 6144 | tf_op jit(solution)/shard_map/psum | solution.py:109
  197.4 0.6 broadcast_in_dim.45
  198.0 78.2 %all-reduce.2.cloned.1.call-done = bf16[1,31,1536]{2,0,1:T(2,128)(2,1)} async-done(((bf16[1,31,1536]{2,0,1:T(2,128)(2,1)}), bf16[1,31,1536]{2,0,1:T(2,128)(2,1)}) %all-reduce.2.cloned.1.call-update) | async-done | bytes 95248 | tf_op jit(solution)/shard_map/psum | solution.py:108
  276.2 1.8 broadcast_in_dim.43
  278.0 0.0 collective-permute-done.2
  278.0 0.0 collective-permute-done.5
  278.0 111.0 %reduce-scatter.2.cloned.1.call-done = bf16[96,1536]{1,0:T(8,128)(2,1)} async-done(((bf16[1536,1536]{1,0:T(8,128)(2,1)}), bf16[96,1536]{1,0:T(8,128)(2,1)}) %reduce-scatter.2.cloned.1.call-update) | async-done | bytes 294928 | tf_op jit(solution)/shard_map/reduce_scatter | solution.py:118
  389.0 1.8 bitcast_convert_fusion
  390.9 0.7 copy.16
  391.6 0.7 copy.17
  (168 shorter events, 0.5 us)
Async XLA Ops:
  7.2 10.6 %copy-start.1 = (bf16[1,128,1536]{2,1,0:T(8,128)(2,1)S(1)}, bf16[1,128,1536]{2,1,0:T(8,128)(2,1)}, u32[]{:S(2)}) copy-start(bf16[1,128,1536]{2,1,0:T(8,128)(2,1)} %param.8) | copy-start | bytes 1179652
  7.2 10.3 %copy-start = (bf16[1,128,1536]{2,1,0:T(8,128)(2,1)S(1)}, bf16[1,128,1536]{2,1,0:T(8,128)(2,1)}, u32[]{:S(2)}) copy-start(bf16[1,128,1536]{2,1,0:T(8,128)(2,1)} %param.9) | copy-start | bytes 1179652
  7.2 118.6 %all-gather.3.cloned.1.call-start = ((), (), s32[]{:S(2)}) async-start(), calls=%async_computation.3 | async-start | bytes 5013504 | tf_op jit(solution)/shard_map/all_gather | solution.py:74
  7.9 268.3 %all-reduce.2.cloned.1.call-start = ((), (), s32[]{:S(2)}) async-start(), calls=%async_computation.2 | async-start | bytes 380928 | tf_op jit(solution)/shard_map/psum | solution.py:108
  17.7 7.8 %copy-start.67 = (f32[128]{0:T(128)}, f32[128]{0:T(128)S(1)}, u32[]{:S(2)}) copy-start(f32[128]{0:T(128)S(1)} %get-tuple-element.84) | copy-start | bytes 1540
  18.2 7.3 %collective-permute-start = (bf16[2,15,1536]{2,1,0:T(8,128)(2,1)S(1)}, bf16[2,15,1536]{2,1,0:T(8,128)(2,1)S(1)}, u32[]{:S(2)}, u32[]{:S(2)}) collective-permute-start(bf16[2,15,1536]{2,1,0:T(8,128)(2,1)S(1)} %get-tuple-element.73), channel_id=1, source_target_pairs={{0,1},{1,2},{2,3},{3,4},{4,5},{5,6},{6,7},{7,8},{8,9},{9,10},{10,1... | collective-permute-start | bytes 276488 | tf_op jit(solution)/shard_map/ppermute | solution.py:16
  22.0 9.5 %collective-permute-start.1 = (bf16[2,15,1536]{2,1,0:T(8,128)(2,1)S(1)}, bf16[2,15,1536]{2,1,0:T(8,128)(2,1)S(1)}, u32[]{:S(2)}, u32[]{:S(2)}) collective-permute-start(bf16[2,15,1536]{2,1,0:T(8,128)(2,1)S(1)} %get-tuple-element.74), channel_id=1, source_target_pairs={{1,0},{2,1},{3,2},{4,3},{5,4},{6,5},{7,6},{8,7},{9,8},{10,9},{11,1... | collective-permute-start | bytes 276488 | tf_op jit(solution)/shard_map/ppermute | solution.py:17
  24.4 7.4 %copy-start.5 = (f32[1536]{0:T(1024)}, f32[1536]{0:T(1024)S(1)}, u32[]{:S(2)}) copy-start(f32[1536]{0:T(1024)S(1)} %get-tuple-element.40) | copy-start | bytes 18436
  24.4 7.4 %copy-start.7 = (f32[1536]{0:T(1024)}, f32[1536]{0:T(1024)S(1)}, u32[]{:S(2)}) copy-start(f32[1536]{0:T(1024)S(1)} %get-tuple-element.41) | copy-start | bytes 18436
  24.4 7.4 %copy-start.9 = (f32[1536]{0:T(1024)}, f32[1536]{0:T(1024)S(1)}, u32[]{:S(2)}) copy-start(f32[1536]{0:T(1024)S(1)} %get-tuple-element.42) | copy-start | bytes 18436
  24.4 7.4 %copy-start.11 = (f32[1536]{0:T(1024)}, f32[1536]{0:T(1024)S(1)}, u32[]{:S(2)}) copy-start(f32[1536]{0:T(1024)S(1)} %get-tuple-element.43) | copy-start | bytes 18436
  24.4 7.4 %copy-start.13 = (f32[1536]{0:T(1024)}, f32[1536]{0:T(1024)S(1)}, u32[]{:S(2)}) copy-start(f32[1536]{0:T(1024)S(1)} %get-tuple-element.44) | copy-start | bytes 18436
  24.4 7.4 %copy-start.15 = (f32[1536]{0:T(1024)}, f32[1536]{0:T(1024)S(1)}, u32[]{:S(2)}) copy-start(f32[1536]{0:T(1024)S(1)} %get-tuple-element.45) | copy-start | bytes 18436
  24.4 7.4 %copy-start.17 = (f32[1536]{0:T(1024)}, f32[1536]{0:T(1024)S(1)}, u32[]{:S(2)}) copy-start(f32[1536]{0:T(1024)S(1)} %get-tuple-element.46) | copy-start | bytes 18436
  24.4 7.4 %copy-start.19 = (f32[1536]{0:T(1024)}, f32[1536]{0:T(1024)S(1)}, u32[]{:S(2)}) copy-start(f32[1536]{0:T(1024)S(1)} %get-tuple-element.47) | copy-start | bytes 18436
  24.5 7.4 %copy-start.21 = (f32[1536]{0:T(1024)}, f32[1536]{0:T(1024)S(1)}, u32[]{:S(2)}) copy-start(f32[1536]{0:T(1024)S(1)} %get-tuple-element.48) | copy-start | bytes 18436
  24.5 7.4 %copy-start.23 = (f32[1536]{0:T(1024)}, f32[1536]{0:T(1024)S(1)}, u32[]{:S(2)}) copy-start(f32[1536]{0:T(1024)S(1)} %get-tuple-element.49) | copy-start | bytes 18436
  24.5 7.4 %copy-start.25 = (f32[1536]{0:T(1024)}, f32[1536]{0:T(1024)S(1)}, u32[]{:S(2)}) copy-start(f32[1536]{0:T(1024)S(1)} %get-tuple-element.50) | copy-start | bytes 18436
  24.5 7.4 %copy-start.27 = (f32[1536]{0:T(1024)}, f32[1536]{0:T(1024)S(1)}, u32[]{:S(2)}) copy-start(f32[1536]{0:T(1024)S(1)} %get-tuple-element.51) | copy-start | bytes 18436
  24.5 7.4 %copy-start.29 = (f32[1536]{0:T(1024)}, f32[1536]{0:T(1024)S(1)}, u32[]{:S(2)}) copy-start(f32[1536]{0:T(1024)S(1)} %get-tuple-element.52) | copy-start | bytes 18436
  24.5 7.4 %copy-start.31 = (f32[1536]{0:T(1024)}, f32[1536]{0:T(1024)S(1)}, u32[]{:S(2)}) copy-start(f32[1536]{0:T(1024)S(1)} %get-tuple-element.53) | copy-start | bytes 18436
  24.5 7.4 %copy-start.33 = (f32[1536]{0:T(1024)}, f32[1536]{0:T(1024)S(1)}, u32[]{:S(2)}) copy-start(f32[1536]{0:T(1024)S(1)} %get-tuple-element.54) | copy-start | bytes 18436
  24.5 7.4 %copy-start.35 = (f32[1536]{0:T(1024)}, f32[1536]{0:T(1024)S(1)}, u32[]{:S(2)}) copy-start(f32[1536]{0:T(1024)S(1)} %get-tuple-element.55) | copy-start | bytes 18436
  24.5 7.4 %copy-start.37 = (f32[1536]{0:T(1024)}, f32[1536]{0:T(1024)S(1)}, u32[]{:S(2)}) copy-start(f32[1536]{0:T(1024)S(1)} %get-tuple-element.56) | copy-start | bytes 18436
  24.5 7.4 %copy-start.39 = (f32[1536]{0:T(1024)}, f32[1536]{0:T(1024)S(1)}, u32[]{:S(2)}) copy-start(f32[1536]{0:T(1024)S(1)} %get-tuple-element.57) | copy-start | bytes 18436
  32.1 93.7 %copy-start.3 = (bf16[1,128,1536]{2,1,0:T(8,128)(2,1)S(1)}, bf16[1,128,1536]{2,1,0:T(8,128)(2,1)}, u32[]{:S(2)}) copy-start(bf16[1,128,1536]{2,1,0:T(8,128)(2,1)} %param.10) | copy-start | bytes 1179652
  140.4 248.7 %reduce-scatter.2.cloned.1.call-start = ((), (), s32[]{:S(2)}) async-start(), calls=%async_computation.1 | async-start | bytes 5013504 | tf_op jit(solution)/shard_map/reduce_scatter | solution.py:118
  144.1 12.3 %collective-permute-start.3 = (bf16[15,1536]{1,0:T(8,128)(2,1)S(1)}, bf16[15,1536]{1,0:T(8,128)(2,1)S(1)}, u32[]{:S(2)}, u32[]{:S(2)}) collective-permute-start(bf16[15,1536]{1,0:T(8,128)(2,1)S(1)} %get-tuple-element.75), channel_id=1, source_target_pairs={{0,1},{1,2},{2,3},{3,4},{4,5},{5,6},{6,7},{7,8},{8,9},{9,10},{10,1... | collective-permute-start | bytes 138248 | tf_op jit(solution)/shard_map/ppermute | solution.py:16
  146.5 10.0 %copy-start.6 = (f32[1536]{0:T(1024)S(1)}, f32[1536]{0:T(1024)}, u32[]{:S(2)}) copy-start(f32[1536]{0:T(1024)} %copy-done.5) | copy-start | bytes 18436
  146.5 10.0 %copy-start.8 = (f32[1536]{0:T(1024)S(1)}, f32[1536]{0:T(1024)}, u32[]{:S(2)}) copy-start(f32[1536]{0:T(1024)} %copy-done.7) | copy-start | bytes 18436
  146.6 10.0 %copy-start.10 = (f32[1536]{0:T(1024)S(1)}, f32[1536]{0:T(1024)}, u32[]{:S(2)}) copy-start(f32[1536]{0:T(1024)} %copy-done.9) | copy-start | bytes 18436
  146.6 10.0 %copy-start.12 = (f32[1536]{0:T(1024)S(1)}, f32[1536]{0:T(1024)}, u32[]{:S(2)}) copy-start(f32[1536]{0:T(1024)} %copy-done.11) | copy-start | bytes 18436
  146.6 10.0 %copy-start.14 = (f32[1536]{0:T(1024)S(1)}, f32[1536]{0:T(1024)}, u32[]{:S(2)}) copy-start(f32[1536]{0:T(1024)} %copy-done.13) | copy-start | bytes 18436
  146.6 10.0 %copy-start.16 = (f32[1536]{0:T(1024)S(1)}, f32[1536]{0:T(1024)}, u32[]{:S(2)}) copy-start(f32[1536]{0:T(1024)} %copy-done.15) | copy-start | bytes 18436
  146.6 10.0 %copy-start.18 = (f32[1536]{0:T(1024)S(1)}, f32[1536]{0:T(1024)}, u32[]{:S(2)}) copy-start(f32[1536]{0:T(1024)} %copy-done.17) | copy-start | bytes 18436
  146.6 10.0 %copy-start.20 = (f32[1536]{0:T(1024)S(1)}, f32[1536]{0:T(1024)}, u32[]{:S(2)}) copy-start(f32[1536]{0:T(1024)} %copy-done.19) | copy-start | bytes 18436
  146.6 10.0 %copy-start.22 = (f32[1536]{0:T(1024)S(1)}, f32[1536]{0:T(1024)}, u32[]{:S(2)}) copy-start(f32[1536]{0:T(1024)} %copy-done.21) | copy-start | bytes 18436
  146.6 10.0 %copy-start.24 = (f32[1536]{0:T(1024)S(1)}, f32[1536]{0:T(1024)}, u32[]{:S(2)}) copy-start(f32[1536]{0:T(1024)} %copy-done.23) | copy-start | bytes 18436
  146.6 10.0 %copy-start.26 = (f32[1536]{0:T(1024)S(1)}, f32[1536]{0:T(1024)}, u32[]{:S(2)}) copy-start(f32[1536]{0:T(1024)} %copy-done.25) | copy-start | bytes 18436
  146.6 10.0 %copy-start.28 = (f32[1536]{0:T(1024)S(1)}, f32[1536]{0:T(1024)}, u32[]{:S(2)}) copy-start(f32[1536]{0:T(1024)} %copy-done.27) | copy-start | bytes 18436
  146.7 10.0 %copy-start.30 = (f32[1536]{0:T(1024)S(1)}, f32[1536]{0:T(1024)}, u32[]{:S(2)}) copy-start(f32[1536]{0:T(1024)} %copy-done.29) | copy-start | bytes 18436
  146.7 10.0 %copy-start.32 = (f32[1536]{0:T(1024)S(1)}, f32[1536]{0:T(1024)}, u32[]{:S(2)}) copy-start(f32[1536]{0:T(1024)} %copy-done.31) | copy-start | bytes 18436
  146.7 10.0 %copy-start.34 = (f32[1536]{0:T(1024)S(1)}, f32[1536]{0:T(1024)}, u32[]{:S(2)}) copy-start(f32[1536]{0:T(1024)} %copy-done.33) | copy-start | bytes 18436
  146.7 10.0 %copy-start.36 = (f32[1536]{0:T(1024)S(1)}, f32[1536]{0:T(1024)}, u32[]{:S(2)}) copy-start(f32[1536]{0:T(1024)} %copy-done.35) | copy-start | bytes 18436
  146.7 10.0 %copy-start.38 = (f32[1536]{0:T(1024)S(1)}, f32[1536]{0:T(1024)}, u32[]{:S(2)}) copy-start(f32[1536]{0:T(1024)} %copy-done.37) | copy-start | bytes 18436
  146.7 10.0 %copy-start.40 = (f32[1536]{0:T(1024)S(1)}, f32[1536]{0:T(1024)}, u32[]{:S(2)}) copy-start(f32[1536]{0:T(1024)} %copy-done.39) | copy-start | bytes 18436
  146.7 10.0 %copy-start.42 = (f32[1536]{0:T(1024)S(1)}, f32[1536]{0:T(1024)}, u32[]{:S(2)}) copy-start(f32[1536]{0:T(1024)} %copy-done.41) | copy-start | bytes 18436
  146.7 10.0 %copy-start.44 = (f32[1536]{0:T(1024)S(1)}, f32[1536]{0:T(1024)}, u32[]{:S(2)}) copy-start(f32[1536]{0:T(1024)} %copy-done.43) | copy-start | bytes 18436
  146.7 10.0 %copy-start.46 = (f32[1536]{0:T(1024)S(1)}, f32[1536]{0:T(1024)}, u32[]{:S(2)}) copy-start(f32[1536]{0:T(1024)} %copy-done.45) | copy-start | bytes 18436
  146.7 10.0 %copy-start.48 = (f32[1536]{0:T(1024)S(1)}, f32[1536]{0:T(1024)}, u32[]{:S(2)}) copy-start(f32[1536]{0:T(1024)} %copy-done.47) | copy-start | bytes 18436
  146.8 10.0 %copy-start.50 = (f32[1536]{0:T(1024)S(1)}, f32[1536]{0:T(1024)}, u32[]{:S(2)}) copy-start(f32[1536]{0:T(1024)} %copy-done.49) | copy-start | bytes 18436
  146.8 10.0 %copy-start.52 = (f32[1536]{0:T(1024)S(1)}, f32[1536]{0:T(1024)}, u32[]{:S(2)}) copy-start(f32[1536]{0:T(1024)} %copy-done.51) | copy-start | bytes 18436
  146.8 10.0 %copy-start.54 = (f32[1536]{0:T(1024)S(1)}, f32[1536]{0:T(1024)}, u32[]{:S(2)}) copy-start(f32[1536]{0:T(1024)} %copy-done.53) | copy-start | bytes 18436
  146.8 10.0 %copy-start.56 = (f32[1536]{0:T(1024)S(1)}, f32[1536]{0:T(1024)}, u32[]{:S(2)}) copy-start(f32[1536]{0:T(1024)} %copy-done.55) | copy-start | bytes 18436
  146.8 10.0 %copy-start.58 = (f32[1536]{0:T(1024)S(1)}, f32[1536]{0:T(1024)}, u32[]{:S(2)}) copy-start(f32[1536]{0:T(1024)} %copy-done.57) | copy-start | bytes 18436
  146.8 10.0 %copy-start.60 = (f32[1536]{0:T(1024)S(1)}, f32[1536]{0:T(1024)}, u32[]{:S(2)}) copy-start(f32[1536]{0:T(1024)} %copy-done.59) | copy-start | bytes 18436
  146.8 10.0 %copy-start.62 = (f32[1536]{0:T(1024)S(1)}, f32[1536]{0:T(1024)}, u32[]{:S(2)}) copy-start(f32[1536]{0:T(1024)} %copy-done.61) | copy-start | bytes 18436
  146.8 10.0 %copy-start.64 = (f32[1536]{0:T(1024)S(1)}, f32[1536]{0:T(1024)}, u32[]{:S(2)}) copy-start(f32[1536]{0:T(1024)} %copy-done.63) | copy-start | bytes 18436
  146.8 10.0 %copy-start.66 = (f32[128]{0:T(128)S(1)}, f32[128]{0:T(128)}, u32[]{:S(2)}) copy-start(f32[128]{0:T(128)} %copy-done.65) | copy-start | bytes 1540
  146.8 10.0 %copy-start.68 = (f32[128]{0:T(128)S(1)}, f32[128]{0:T(128)}, u32[]{:S(2)}) copy-start(f32[128]{0:T(128)} %copy-done.67) | copy-start | bytes 1540
  146.9 10.0 %copy-start.70 = (f32[128]{0:T(128)S(1)}, f32[128]{0:T(128)}, u32[]{:S(2)}) copy-start(f32[128]{0:T(128)} %copy-done.69) | copy-start | bytes 1540
  146.9 9.6 %collective-permute-start.4 = (bf16[15,1536]{1,0:T(8,128)(2,1)S(1)}, bf16[15,1536]{1,0:T(8,128)(2,1)S(1)}, u32[]{:S(2)}, u32[]{:S(2)}) collective-permute-start(bf16[15,1536]{1,0:T(8,128)(2,1)S(1)} %get-tuple-element.76), channel_id=1, source_target_pairs={{1,0},{2,1},{3,2},{4,3},{5,4},{6,5},{7,6},{8,7},{9,8},{10,9},{11,1... | collective-permute-start | bytes 138248 | tf_op jit(solution)/shard_map/ppermute | solution.py:17
  154.3 123.7 %collective-permute-start.2 = (bf16[1,128,1536]{2,1,0:T(8,128)(2,1)}, bf16[1,128,1536]{2,1,0:T(8,128)(2,1)S(1)}, u32[]{:S(2)}, u32[]{:S(2)}) collective-permute-start(bf16[1,128,1536]{2,1,0:T(8,128)(2,1)} %fusion.17), channel_id=1, source_target_pairs={{0,16},{16,32},{32,48},{48,64},{64,80},{80,96},{96,112},{112,128},... | collective-permute-start | bytes 1179656 | tf_op jit(solution)/shard_map/ppermute | solution.py:25
  162.4 115.6 %collective-permute-start.5 = (bf16[1,128,1536]{2,1,0:T(8,128)(2,1)S(1)}, bf16[1,128,1536]{2,1,0:T(8,128)(2,1)S(1)}, u32[]{:S(2)}, u32[]{:S(2)}) collective-permute-start(bf16[1,128,1536]{2,1,0:T(8,128)(2,1)S(1)} %fusion.141), channel_id=1, source_target_pairs={{16,0},{32,16},{48,32},{64,48},{80,64},{96,80},{112,96},{128,112},... | collective-permute-start | bytes 1179656 | tf_op jit(solution)/shard_map/ppermute | solution.py:25
  (16 other events, 111.3 us)
Sparse Core Ops, SparseCore 0:
  9.8 115.9 all-gather.2
  140.5 135.6 all-reduce.1
  278.8 110.2 reduce-scatter.1
where the time goes:
time: 400 us; the launch traced here: 399 us
  waiting for transfers between devices  283 us (71%)
  blocking collectives  31.3 us (8%)
  other arithmetic  27.8 us (7%)
  starting transfers between devices  17.7 us (4%)
  between operations  15.3 us (4%)
  matrix products  13 us (3%)
  local copies, waits for them, and re-layouts  10.5 us (3%)
    reduce_scatter x1, waiting for transfers between devices, per_device(): lax.psum_scatter(lax.optimization_barrier(partial_value.astype(jnp.bfloat...  111 us
    all_gather x1, waiting for transfers between devices, per_device(): lax.all_gather(w_rows, 'tm', axis=0, tiled=True)  86.8 us
    psum x1, waiting for transfers between devices, per_device(): lax.psum(kernel_local.astype(jnp.bfloat16), 'tm').astype(jnp.float32)  78.2 us
    psum x1, blocking collectives, per_device(): lax.psum(gain_local.astype(jnp.bfloat16), 'tm').astype(jnp.float32)  31.3 us
  transfers between devices with their start and end apart: 9, of which 5 were waited for; matrix products, arithmetic and copies ran while one was open for 8% of the time, Pallas kernels for 0%

commit v1 on v0

--- a/solution.py
+++ b/solution.py
@@ -71,7 +71,9 @@
     columns = hidden_fwd
     product = jnp.dot(
         columns,
-        lax.all_gather(w_rows, "tm", axis=0, tiled=True),
+        jnp.concatenate(
+            lax.all_to_all(jnp.stack([w_rows] * lax.axis_size("tm")), "tm", 0, 0), axis=0
+        ),
         preferred_element_type=jnp.float32,
     )
     hidden_grad = lax.dot_general(

time: 400 us -> 477 us (1.19)
  waiting for transfers between devices: 283 us -> 350 us
  starting transfers between devices: 17.7 us -> 29.1 us
    ppermute x2, waiting for transfers between devices: 5.99 us -> 121 us  [extended(): after = lax.ppermute(first, axis, down)]
    all_gather x1, waiting for transfers between devices: 86.8 us -> 29.4 us  [per_device(): lax.all_gather(w_rows, 'tm', axis=0, tiled=True)]
    all_to_all x0 -> x1, starting transfers between devices: none -> 9.63 us  [per_device(): lax.all_to_all(jnp.stack([w_rows] * lax.axis_size('tm')), 'tm', 0, 0)]
    ppermute x2, waiting for transfers between devices: 0.62 us -> 9.4 us  [extended(): before = lax.ppermute(last, axis, up)]
  transfers between devices with their start and end apart: 9 -> 10, of which waited for: 5 -> 5; matrix products, arithmetic and copies ran while one was open for 8% -> 10% of each run, Pallas kernels for 0% -> 0%
where the time goes in v1:
time: 477 us; the launch traced here: 476 us
  waiting for transfers between devices  350 us (73%)
  blocking collectives  31.5 us (7%)
  starting transfers between devices  29.1 us (6%)
  other arithmetic  23.4 us (5%)
  between operations  15.2 us (3%)
  local copies, waits for them, and re-layouts  14.1 us (3%)
  matrix products  13.1 us (3%)
    ppermute x2, waiting for transfers between devices, extended(): after = lax.ppermute(first, axis, down)  121 us
    reduce_scatter x1, waiting for transfers between devices, per_device(): lax.psum_scatter(lax.optimization_barrier(partial_value.astype(jnp.bfloat...  111 us
    psum x1, waiting for transfers between devices, per_device(): lax.psum(kernel_local.astype(jnp.bfloat16), 'tm').astype(jnp.float32)  78.6 us
    psum x1, blocking collectives, per_device(): lax.psum(gain_local.astype(jnp.bfloat16), 'tm').astype(jnp.float32)  31.5 us
    all_gather x1, waiting for transfers between devices, per_device(): lax.all_gather(w_rows, 'tm', axis=0, tiled=True)  29.4 us
    all_to_all x1, starting transfers between devices, per_device(): lax.all_to_all(jnp.stack([w_rows] * lax.axis_size('tm')), 'tm', 0, 0)  9.63 us
  transfers between devices with their start and end apart: 10, of which 5 were waited for; matrix products, arithmetic and copies ran while one was open for 10% of the time, Pallas kernels for 0%

profile of v1, /device:TPU:42, one launch (start us, length us, event | category | flops | bytes accessed | tf_op | source)
XLA Modules:
  0.0 476.2 jit_solution(6674409074623461309)
XLA Ops:
  7.2 0.0 all-gather.3.cloned.1.call-start
  7.2 0.7 all-gather.3.cloned.1.call-update
  7.9 3.6 stack.105
  11.5 0.0 copy-start.1
  11.5 9.6 %all-to-all-start = ((bf16[16,96,1536]{2,1,0:T(8,128)(2,1)}), bf16[16,96,1536]{2,1,0:T(8,128)(2,1)}, u32[]{:S(2)}, u32[]{:S(2)}) async-start(bf16[16,96,1536]{2,1,0:T(8,128)(2,1)} %stack.105), calls=%async_computation | async-start | bytes 9437184 | tf_op jit(solution)/shard_map/all_to_all | solution.py:75
  21.1 0.0 all-reduce.2.cloned.1.call-start
  21.2 0.6 fusion.143
  21.8 1.9 fusion.137
  23.8 1.3 compare_convert_fusion
  25.1 0.1 convert_reduce_fusion
  25.2 0.1 convert_reduce_fusion.1
  25.4 0.3 fusion.64
  25.6 0.3 fusion.43
  25.9 0.4 fusion.47
  26.3 0.1 copy-done.67
  26.4 2.5 collective-permute-start.1
  28.9 4.3 collective-permute-start
  33.2 0.3 slice_reduce_fusion.30
  33.7 0.2 slice_reduce_fusion.29
  34.0 0.0 copy-start.61
  34.0 120.7 %collective-permute-done.1 = bf16[2,15,1536]{2,1,0:T(8,128)(2,1)S(1)} collective-permute-done((bf16[2,15,1536]{2,1,0:T(8,128)(2,1)S(1)}, bf16[2,15,1536]{2,1,0:T(8,128)(2,1)S(1)}, u32[]{:S(2)}, u32[]{:S(2)}) %collective-permute-start.1) | collective-permute-done | bytes 92192 | tf_op jit(solution)/shard_map/ppermute | solution.py:17
  154.7 9.4 %collective-permute-done = bf16[2,15,1536]{2,1,0:T(8,128)(2,1)S(1)} collective-permute-done((bf16[2,15,1536]{2,1,0:T(8,128)(2,1)S(1)}, bf16[2,15,1536]{2,1,0:T(8,128)(2,1)S(1)}, u32[]{:S(2)}, u32[]{:S(2)}) %collective-permute-start) | collective-permute-done | bytes 92192 | tf_op jit(solution)/shard_map/ppermute | solution.py:16
  164.1 0.3 maximum_convert_fusion
  164.5 0.0 copy-start.3
  164.6 6.8 %fusion.11 = f32[2,128,1536]{2,1,0:T(8,128)} fusion(f32[2,158,1536]{2,1,0:T(8,128)S(1)} %maximum_convert_fusion, f32[1536]{0:T(1024)S(1)} %get-tuple-element.68, f32[1536]{0:T(1024)S(1)} %get-tuple-element.69, f32[1536]{0:T(1024)S(1)} %get-tuple-element.40, f32[1536]{0:T(1024)S(1)} %get-tuple-element.41, f32[1536]{0:T(1024)S(1)} %get-tuple-element.42, ...), kind=kLoop, calls=%fused_computation.41 | loop fusion | flops 23986176 | bytes 50522112 | tf_op jit(solution)/shard_map/add | solution.py:41
  171.5 29.4 %all-gather.3.cloned.1.call-done = bf16[1,1536,1536]{2,1,0:T(8,128)(2,1)} async-done(((bf16[1,96,1536]{2,1,0:T(8,128)(2,1)}), bf16[1,1536,1536]{2,1,0:T(8,128)(2,1)}) %all-gather.3.cloned.1.call-update) | async-done | bytes 4718608 | tf_op jit(solution)/shard_map/all_gather | solution.py:81
  200.9 5.5 %fusion.94 = (f32[1536]{0:T(1024)S(1)}, f32[1536]{0:T(1024)S(1)}, f32[1536]{0:T(1024)S(1)}, f32[1536]{0:T(1024)S(1)}, f32[1536]{0:T(1024)S(1)}, /*index=5*/f32[1...) fusion(f32[2,158,1536]{2,1,0:T(8,128)S(1)} %maximum_convert_fus, ...), kind=kOutput, calls=%fused_computation.161 | convolution fusion | flops 611037696 | bytes 16594944 | tf_op jit(solution)/shard_map/dot_general | solution.py:79
  206.3 0.6 stack.106
  206.9 2.0 fusion.95
  209.3 0.6 stack.131
  209.9 0.6 stack.132
  210.5 0.6 stack.133
  211.1 0.6 stack.134
  211.7 0.6 stack.135
  212.3 0.6 stack.136
  212.9 1.8 stack.137
  214.7 0.8 broadcast_in_dim.42
  215.5 0.0 all-reduce.2.cloned.1.call-update
  215.5 0.0 reduce-scatter.2.cloned.1.call-start
  215.6 3.6 fusion
  219.2 0.0 reduce-scatter.2.cloned.1.call-update
  219.2 0.6 fusion.142
  219.9 1.9 collective-permute-start.4
  221.8 5.2 %collective-permute-start.3 = (bf16[15,1536]{1,0:T(8,128)(2,1)S(1)}, bf16[15,1536]{1,0:T(8,128)(2,1)S(1)}, u32[]{:S(2)}, u32[]{:S(2)}) collective-permute-start(bf16[15,1536]{1,0:T(8,128)(2,1)S(1)} %get-tuple-element.75), channel_id=1, source_target_pairs={{0,1},{1,2},{2,3},{3,4},{4,5},{5,6},{6,7},{7,8},{8,9},{9,10},{10,1... | collective-permute-start | bytes 138248 | tf_op jit(solution)/shard_map/ppermute | solution.py:16
  227.0 0.0 all-to-all-done
  227.3 0.0 copy-start.62
  227.3 3.9 fusion.10
  231.3 1.9 collective-permute-start.2
  233.2 0.0 collective-permute-done.4
  233.2 0.0 collective-permute-done.3
  233.2 0.1 maximum_convert_fusion.1
  233.7 5.1 %fusion.63 = (f32[1536]{0:T(1024)S(1)}, f32[128]{0:T(128)S(1)}, f32[128]{0:T(128)S(1)}, f32[128,1536]{1,0:T(8,128)S(1)}) fusion(bf16[1,128,1536]{2,1,0:T(8,128)(2,1)S(1)} %copy-done, f32[128]{0:T(128)S(1)} %copy-done.68, f32[128]{0:T(128)S(1)} %copy-done.66, f32[1536]{0:T(1024)S(1)} %reduce.3, f32[128]{0:T(128)S(1)} %copy-done.71, ...), kind=kLoop, calls=%fused_computation.130 | loop fusion | flops 13957376 | bytes 25764352 | tf_op jit(solution)/shard_map/reduce_sum | solution.py:108
  238.8 0.4 fusion.132
  239.2 3.6 collective-permute-start.5
  242.8 31.5 %psum.15 = bf16[1,1536]{1,0:T(2,128)(2,1)S(1)} all-reduce(bf16[1,1536]{1,0:T(2,128)(2,1)S(1)} %broadcast_in_dim.44), channel_id=1, replica_groups=mesh['section'=16,'tm'=16] {'tm'}, use_global_device_ids=true, to_apply=%region_42.43 | all-reduce | flops 1536 | bytes 6144 | tf_op jit(solution)/shard_map/psum | solution.py:111
  274.3 0.6 broadcast_in_dim.45
  274.9 78.6 %all-reduce.2.cloned.1.call-done = bf16[1,31,1536]{2,0,1:T(2,128)(2,1)} async-done(((bf16[1,31,1536]{2,0,1:T(2,128)(2,1)}), bf16[1,31,1536]{2,0,1:T(2,128)(2,1)}) %all-reduce.2.cloned.1.call-update) | async-done | bytes 95248 | tf_op jit(solution)/shard_map/psum | solution.py:110
  353.5 1.8 broadcast_in_dim.43
  355.3 0.0 collective-permute-done.2
  355.3 0.0 collective-permute-done.5
  355.3 111.0 %reduce-scatter.2.cloned.1.call-done = bf16[96,1536]{1,0:T(8,128)(2,1)} async-done(((bf16[1536,1536]{1,0:T(8,128)(2,1)}), bf16[96,1536]{1,0:T(8,128)(2,1)}) %reduce-scatter.2.cloned.1.call-update) | async-done | bytes 294928 | tf_op jit(solution)/shard_map/reduce_scatter | solution.py:120
  466.3 1.8 bitcast_convert_fusion
  468.1 0.7 copy.16
  468.9 0.7 copy.17
  (177 shorter events, 0.5 us)
Async XLA Ops:
  7.2 193.7 %all-gather.3.cloned.1.call-start = ((), (), s32[]{:S(2)}) async-start(), calls=%async_computation.4 | async-start | bytes 5013504 | tf_op jit(solution)/shard_map/all_gather | solution.py:81
  11.5 9.7 %copy-start.69 = (f32[1,1536]{1,0:T(1,128)S(1)}, f32[1,1536]{1,0:T(1,128)}, u32[]{:S(2)}) copy-start(f32[1,1536]{1,0:T(1,128)} %param.11) | copy-start | bytes 18436
  11.5 9.7 %copy-start.72 = (s32[1,2]{1,0:T(1,128)S(1)}, s32[1,2]{1,0:T(1,128)}, u32[]{:S(2)}) copy-start(s32[1,2]{1,0:T(1,128)} %param.15) | copy-start | bytes 28
  11.5 10.3 %copy-start.73 = (s32[32]{0:T(128)S(1)}, s32[32]{0:T(128)}, u32[]{:S(2)}) copy-start(s32[32]{0:T(128)} %param.14) | copy-start | bytes 388
  11.5 13.6 %copy-start = (bf16[1,128,1536]{2,1,0:T(8,128)(2,1)S(1)}, bf16[1,128,1536]{2,1,0:T(8,128)(2,1)}, u32[]{:S(2)}) copy-start(bf16[1,128,1536]{2,1,0:T(8,128)(2,1)} %param.9) | copy-start | bytes 1179652
  11.5 13.7 %copy-start.1 = (bf16[1,128,1536]{2,1,0:T(8,128)(2,1)S(1)}, bf16[1,128,1536]{2,1,0:T(8,128)(2,1)}, u32[]{:S(2)}) copy-start(bf16[1,128,1536]{2,1,0:T(8,128)(2,1)} %param.8) | copy-start | bytes 1179652
  11.5 215.5 %all-to-all-start = ((bf16[16,96,1536]{2,1,0:T(8,128)(2,1)}), bf16[16,96,1536]{2,1,0:T(8,128)(2,1)}, u32[]{:S(2)}, u32[]{:S(2)}) async-start(bf16[16,96,1536]{2,1,0:T(8,128)(2,1)} %stack.105), calls=%async_computation | async-start | bytes 9437184 | tf_op jit(solution)/shard_map/all_to_all | solution.py:75
  21.1 332.4 %all-reduce.2.cloned.1.call-start = ((), (), s32[]{:S(2)}) async-start(), calls=%async_computation.3 | async-start | bytes 380928 | tf_op jit(solution)/shard_map/psum | solution.py:110
  25.6 7.6 %copy-start.4 = (f32[1,31,1536]{2,0,1:T(1,128)S(1)}, f32[1,31,1536]{2,0,1:T(1,128)}, u32[]{:S(2)}) copy-start(f32[1,31,1536]{2,0,1:T(1,128)} %param.12) | copy-start | bytes 571396
  26.4 128.3 %collective-permute-start.1 = (bf16[2,15,1536]{2,1,0:T(8,128)(2,1)S(1)}, bf16[2,15,1536]{2,1,0:T(8,128)(2,1)S(1)}, u32[]{:S(2)}, u32[]{:S(2)}) collective-permute-start(bf16[2,15,1536]{2,1,0:T(8,128)(2,1)S(1)} %get-tuple-element.74), channel_id=1, source_target_pairs={{1,0},{2,1},{3,2},{4,3},{5,4},{6,5},{7,6},{8,7},{9,8},{10,9},{11,1... | collective-permute-start | bytes 276488 | tf_op jit(solution)/shard_map/ppermute | solution.py:17
  28.9 135.2 %collective-permute-start = (bf16[2,15,1536]{2,1,0:T(8,128)(2,1)S(1)}, bf16[2,15,1536]{2,1,0:T(8,128)(2,1)S(1)}, u32[]{:S(2)}, u32[]{:S(2)}) collective-permute-start(bf16[2,15,1536]{2,1,0:T(8,128)(2,1)S(1)} %get-tuple-element.73), channel_id=1, source_target_pairs={{0,1},{1,2},{2,3},{3,4},{4,5},{5,6},{6,7},{7,8},{8,9},{9,10},{10,1... | collective-permute-start | bytes 276488 | tf_op jit(solution)/shard_map/ppermute | solution.py:16
  33.5 130.9 %copy-start.5 = (f32[1536]{0:T(1024)}, f32[1536]{0:T(1024)S(1)}, u32[]{:S(2)}) copy-start(f32[1536]{0:T(1024)S(1)} %get-tuple-element.40) | copy-start | bytes 18436
  33.5 130.9 %copy-start.7 = (f32[1536]{0:T(1024)}, f32[1536]{0:T(1024)S(1)}, u32[]{:S(2)}) copy-start(f32[1536]{0:T(1024)S(1)} %get-tuple-element.41) | copy-start | bytes 18436
  33.5 130.9 %copy-start.9 = (f32[1536]{0:T(1024)}, f32[1536]{0:T(1024)S(1)}, u32[]{:S(2)}) copy-start(f32[1536]{0:T(1024)S(1)} %get-tuple-element.42) | copy-start | bytes 18436
  33.5 130.9 %copy-start.11 = (f32[1536]{0:T(1024)}, f32[1536]{0:T(1024)S(1)}, u32[]{:S(2)}) copy-start(f32[1536]{0:T(1024)S(1)} %get-tuple-element.43) | copy-start | bytes 18436
  33.6 130.9 %copy-start.13 = (f32[1536]{0:T(1024)}, f32[1536]{0:T(1024)S(1)}, u32[]{:S(2)}) copy-start(f32[1536]{0:T(1024)S(1)} %get-tuple-element.44) | copy-start | bytes 18436
  33.6 130.9 %copy-start.15 = (f32[1536]{0:T(1024)}, f32[1536]{0:T(1024)S(1)}, u32[]{:S(2)}) copy-start(f32[1536]{0:T(1024)S(1)} %get-tuple-element.45) | copy-start | bytes 18436
  33.6 130.9 %copy-start.17 = (f32[1536]{0:T(1024)}, f32[1536]{0:T(1024)S(1)}, u32[]{:S(2)}) copy-start(f32[1536]{0:T(1024)S(1)} %get-tuple-element.46) | copy-start | bytes 18436
  33.6 130.9 %copy-start.19 = (f32[1536]{0:T(1024)}, f32[1536]{0:T(1024)S(1)}, u32[]{:S(2)}) copy-start(f32[1536]{0:T(1024)S(1)} %get-tuple-element.47) | copy-start | bytes 18436
  33.6 130.9 %copy-start.21 = (f32[1536]{0:T(1024)}, f32[1536]{0:T(1024)S(1)}, u32[]{:S(2)}) copy-start(f32[1536]{0:T(1024)S(1)} %get-tuple-element.48) | copy-start | bytes 18436
  33.6 130.9 %copy-start.23 = (f32[1536]{0:T(1024)}, f32[1536]{0:T(1024)S(1)}, u32[]{:S(2)}) copy-start(f32[1536]{0:T(1024)S(1)} %get-tuple-element.49) | copy-start | bytes 18436
  33.6 130.9 %copy-start.25 = (f32[1536]{0:T(1024)}, f32[1536]{0:T(1024)S(1)}, u32[]{:S(2)}) copy-start(f32[1536]{0:T(1024)S(1)} %get-tuple-element.50) | copy-start | bytes 18436
  33.6 130.9 %copy-start.27 = (f32[1536]{0:T(1024)}, f32[1536]{0:T(1024)S(1)}, u32[]{:S(2)}) copy-start(f32[1536]{0:T(1024)S(1)} %get-tuple-element.51) | copy-start | bytes 18436
  33.6 130.9 %copy-start.29 = (f32[1536]{0:T(1024)}, f32[1536]{0:T(1024)S(1)}, u32[]{:S(2)}) copy-start(f32[1536]{0:T(1024)S(1)} %get-tuple-element.52) | copy-start | bytes 18436
  33.6 130.9 %copy-start.31 = (f32[1536]{0:T(1024)}, f32[1536]{0:T(1024)S(1)}, u32[]{:S(2)}) copy-start(f32[1536]{0:T(1024)S(1)} %get-tuple-element.53) | copy-start | bytes 18436
  33.7 130.9 %copy-start.33 = (f32[1536]{0:T(1024)}, f32[1536]{0:T(1024)S(1)}, u32[]{:S(2)}) copy-start(f32[1536]{0:T(1024)S(1)} %get-tuple-element.54) | copy-start | bytes 18436
  33.7 130.9 %copy-start.35 = (f32[1536]{0:T(1024)}, f32[1536]{0:T(1024)S(1)}, u32[]{:S(2)}) copy-start(f32[1536]{0:T(1024)S(1)} %get-tuple-element.55) | copy-start | bytes 18436
  33.7 130.9 %copy-start.37 = (f32[1536]{0:T(1024)}, f32[1536]{0:T(1024)S(1)}, u32[]{:S(2)}) copy-start(f32[1536]{0:T(1024)S(1)} %get-tuple-element.56) | copy-start | bytes 18436
  33.7 130.9 %copy-start.39 = (f32[1536]{0:T(1024)}, f32[1536]{0:T(1024)S(1)}, u32[]{:S(2)}) copy-start(f32[1536]{0:T(1024)S(1)} %get-tuple-element.57) | copy-start | bytes 18436
  33.9 137.5 %copy-start.41 = (f32[1536]{0:T(1024)}, f32[1536]{0:T(1024)S(1)}, u32[]{:S(2)}) copy-start(f32[1536]{0:T(1024)S(1)} %get-tuple-element.58) | copy-start | bytes 18436
  33.9 137.5 %copy-start.43 = (f32[1536]{0:T(1024)}, f32[1536]{0:T(1024)S(1)}, u32[]{:S(2)}) copy-start(f32[1536]{0:T(1024)S(1)} %get-tuple-element.59) | copy-start | bytes 18436
  33.9 137.5 %copy-start.45 = (f32[1536]{0:T(1024)}, f32[1536]{0:T(1024)S(1)}, u32[]{:S(2)}) copy-start(f32[1536]{0:T(1024)S(1)} %get-tuple-element.60) | copy-start | bytes 18436
  33.9 137.5 %copy-start.47 = (f32[1536]{0:T(1024)}, f32[1536]{0:T(1024)S(1)}, u32[]{:S(2)}) copy-start(f32[1536]{0:T(1024)S(1)} %get-tuple-element.61) | copy-start | bytes 18436
  33.9 137.5 %copy-start.49 = (f32[1536]{0:T(1024)}, f32[1536]{0:T(1024)S(1)}, u32[]{:S(2)}) copy-start(f32[1536]{0:T(1024)S(1)} %get-tuple-element.62) | copy-start | bytes 18436
  33.9 137.5 %copy-start.51 = (f32[1536]{0:T(1024)}, f32[1536]{0:T(1024)S(1)}, u32[]{:S(2)}) copy-start(f32[1536]{0:T(1024)S(1)} %get-tuple-element.63) | copy-start | bytes 18436
  34.0 137.5 %copy-start.53 = (f32[1536]{0:T(1024)}, f32[1536]{0:T(1024)S(1)}, u32[]{:S(2)}) copy-start(f32[1536]{0:T(1024)S(1)} %get-tuple-element.64) | copy-start | bytes 18436
  34.0 137.5 %copy-start.55 = (f32[1536]{0:T(1024)}, f32[1536]{0:T(1024)S(1)}, u32[]{:S(2)}) copy-start(f32[1536]{0:T(1024)S(1)} %get-tuple-element.65) | copy-start | bytes 18436
  34.0 137.5 %copy-start.57 = (f32[1536]{0:T(1024)}, f32[1536]{0:T(1024)S(1)}, u32[]{:S(2)}) copy-start(f32[1536]{0:T(1024)S(1)} %get-tuple-element.66) | copy-start | bytes 18436
  34.0 137.5 %copy-start.59 = (f32[1536]{0:T(1024)}, f32[1536]{0:T(1024)S(1)}, u32[]{:S(2)}) copy-start(f32[1536]{0:T(1024)S(1)} %get-tuple-element.67) | copy-start | bytes 18436
  34.0 137.5 %copy-start.61 = (f32[1536]{0:T(1024)}, f32[1536]{0:T(1024)S(1)}, u32[]{:S(2)}) copy-start(f32[1536]{0:T(1024)S(1)} %get-tuple-element.68) | copy-start | bytes 18436
  34.0 137.5 %copy-start.63 = (f32[1536]{0:T(1024)}, f32[1536]{0:T(1024)S(1)}, u32[]{:S(2)}) copy-start(f32[1536]{0:T(1024)S(1)} %get-tuple-element.69) | copy-start | bytes 18436
  164.5 36.3 %copy-start.3 = (bf16[1,128,1536]{2,1,0:T(8,128)(2,1)S(1)}, bf16[1,128,1536]{2,1,0:T(8,128)(2,1)}, u32[]{:S(2)}) copy-start(bf16[1,128,1536]{2,1,0:T(8,128)(2,1)} %param.10) | copy-start | bytes 1179652
  208.9 6.6 %copy-start.2 = (f32[2,128,1536]{2,1,0:T(8,128)S(1)}, f32[2,128,1536]{2,1,0:T(8,128)}, u32[]{:S(2)}) copy-start(f32[2,128,1536]{2,1,0:T(8,128)} %fusion.11) | copy-start | bytes 4718596
  215.5 250.8 %reduce-scatter.2.cloned.1.call-start = ((), (), s32[]{:S(2)}) async-start(), calls=%async_computation.2 | async-start | bytes 5013504 | tf_op jit(solution)/shard_map/reduce_scatter | solution.py:120
  219.9 13.3 %collective-permute-start.4 = (bf16[15,1536]{1,0:T(8,128)(2,1)}, bf16[15,1536]{1,0:T(8,128)(2,1)S(1)}, u32[]{:S(2)}, u32[]{:S(2)}) collective-permute-start(bf16[15,1536]{1,0:T(8,128)(2,1)} %get-tuple-element.76), channel_id=1, source_target_pairs={{1,0},{2,1},{3,2},{4,3},{5,4},{6,5},{7,6},{8,7},{9,8},{10,9},{11,1... | collective-permute-start | bytes 138248 | tf_op jit(solution)/shard_map/ppermute | solution.py:17
  221.8 11.4 %collective-permute-start.3 = (bf16[15,1536]{1,0:T(8,128)(2,1)S(1)}, bf16[15,1536]{1,0:T(8,128)(2,1)S(1)}, u32[]{:S(2)}, u32[]{:S(2)}) collective-permute-start(bf16[15,1536]{1,0:T(8,128)(2,1)S(1)} %get-tuple-element.75), channel_id=1, source_target_pairs={{0,1},{1,2},{2,3},{3,4},{4,5},{5,6},{6,7},{7,8},{8,9},{9,10},{10,1... | collective-permute-start | bytes 138248 | tf_op jit(solution)/shard_map/ppermute | solution.py:16
  227.0 6.4 %copy-start.6 = (f32[1536]{0:T(1024)S(1)}, f32[1536]{0:T(1024)}, u32[]{:S(2)}) copy-start(f32[1536]{0:T(1024)} %copy-done.5) | copy-start | bytes 18436
  227.0 6.4 %copy-start.8 = (f32[1536]{0:T(1024)S(1)}, f32[1536]{0:T(1024)}, u32[]{:S(2)}) copy-start(f32[1536]{0:T(1024)} %copy-done.7) | copy-start | bytes 18436
  227.0 6.4 %copy-start.10 = (f32[1536]{0:T(1024)S(1)}, f32[1536]{0:T(1024)}, u32[]{:S(2)}) copy-start(f32[1536]{0:T(1024)} %copy-done.9) | copy-start | bytes 18436
  227.0 6.4 %copy-start.12 = (f32[1536]{0:T(1024)S(1)}, f32[1536]{0:T(1024)}, u32[]{:S(2)}) copy-start(f32[1536]{0:T(1024)} %copy-done.11) | copy-start | bytes 18436
  227.0 6.4 %copy-start.14 = (f32[1536]{0:T(1024)S(1)}, f32[1536]{0:T(1024)}, u32[]{:S(2)}) copy-start(f32[1536]{0:T(1024)} %copy-done.13) | copy-start | bytes 18436
  227.0 6.4 %copy-start.16 = (f32[1536]{0:T(1024)S(1)}, f32[1536]{0:T(1024)}, u32[]{:S(2)}) copy-start(f32[1536]{0:T(1024)} %copy-done.15) | copy-start | bytes 18436
  227.0 6.4 %copy-start.18 = (f32[1536]{0:T(1024)S(1)}, f32[1536]{0:T(1024)}, u32[]{:S(2)}) copy-start(f32[1536]{0:T(1024)} %copy-done.17) | copy-start | bytes 18436
  227.0 6.4 %copy-start.20 = (f32[1536]{0:T(1024)S(1)}, f32[1536]{0:T(1024)}, u32[]{:S(2)}) copy-start(f32[1536]{0:T(1024)} %copy-done.19) | copy-start | bytes 18436
  227.1 6.4 %copy-start.22 = (f32[1536]{0:T(1024)S(1)}, f32[1536]{0:T(1024)}, u32[]{:S(2)}) copy-start(f32[1536]{0:T(1024)} %copy-done.21) | copy-start | bytes 18436
  227.1 6.4 %copy-start.24 = (f32[1536]{0:T(1024)S(1)}, f32[1536]{0:T(1024)}, u32[]{:S(2)}) copy-start(f32[1536]{0:T(1024)} %copy-done.23) | copy-start | bytes 18436
  227.1 6.4 %copy-start.26 = (f32[1536]{0:T(1024)S(1)}, f32[1536]{0:T(1024)}, u32[]{:S(2)}) copy-start(f32[1536]{0:T(1024)} %copy-done.25) | copy-start | bytes 18436
  227.1 6.4 %copy-start.28 = (f32[1536]{0:T(1024)S(1)}, f32[1536]{0:T(1024)}, u32[]{:S(2)}) copy-start(f32[1536]{0:T(1024)} %copy-done.27) | copy-start | bytes 18436
  227.1 6.4 %copy-start.30 = (f32[1536]{0:T(1024)S(1)}, f32[1536]{0:T(1024)}, u32[]{:S(2)}) copy-start(f32[1536]{0:T(1024)} %copy-done.29) | copy-start | bytes 18436
  227.1 6.4 %copy-start.32 = (f32[1536]{0:T(1024)S(1)}, f32[1536]{0:T(1024)}, u32[]{:S(2)}) copy-start(f32[1536]{0:T(1024)} %copy-done.31) | copy-start | bytes 18436
  227.1 6.4 %copy-start.34 = (f32[1536]{0:T(1024)S(1)}, f32[1536]{0:T(1024)}, u32[]{:S(2)}) copy-start(f32[1536]{0:T(1024)} %copy-done.33) | copy-start | bytes 18436
  227.1 6.4 %copy-start.36 = (f32[1536]{0:T(1024)S(1)}, f32[1536]{0:T(1024)}, u32[]{:S(2)}) copy-start(f32[1536]{0:T(1024)} %copy-done.35) | copy-start | bytes 18436
  231.3 124.0 %collective-permute-start.2 = (bf16[1,128,1536]{2,1,0:T(8,128)(2,1)}, bf16[1,128,1536]{2,1,0:T(8,128)(2,1)S(1)}, u32[]{:S(2)}, u32[]{:S(2)}) collective-permute-start(bf16[1,128,1536]{2,1,0:T(8,128)(2,1)} %fusion.10), channel_id=1, source_target_pairs={{0,16},{16,32},{32,48},{48,64},{64,80},{80,96},{96,112},{112,128},... | collective-permute-start | bytes 1179656 | tf_op jit(solution)/shard_map/ppermute | solution.py:25
  239.2 116.1 %collective-permute-start.5 = (bf16[1,128,1536]{2,1,0:T(8,128)(2,1)S(1)}, bf16[1,128,1536]{2,1,0:T(8,128)(2,1)S(1)}, u32[]{:S(2)}, u32[]{:S(2)}) collective-permute-start(bf16[1,128,1536]{2,1,0:T(8,128)(2,1)S(1)} %fusion.132), channel_id=1, source_target_pairs={{16,0},{32,16},{48,32},{64,48},{80,64},{96,80},{112,96},{128,112},... | collective-permute-start | bytes 1179656 | tf_op jit(solution)/shard_map/ppermute | solution.py:25
  (20 other events, 110.8 us)
Sparse Core Ops, SparseCore 0:
  9.8 191.0 all-gather.2
  215.6 137.8 all-reduce.1
  356.1 110.2 reduce-scatter.1
